TPU v7x, 32 devices: a whole 2x2x4 slice. The times are simulated.
32 devices in a mesh: dp: 2 (over core), context: 4 (over y, x), tensor: 4 (over z).
Axes of the slice: x: 2, y: 2, z: 4, core: 2. Of those that a mesh axis runs over, the one named last changes fastest.
Arguments:
- inputs: bfloat16 [3072, 1024], P(('dp', 'context')), may hold values from -6 to 6
- cotangent: bfloat16 [3072, 1024], P(('dp', 'context')), may hold values from -6 to 6
- initial_state: float32 [2, 4, 128, 256], P('dp', 'tensor'), may hold values from -6 to 6
- norm_one: float32 [1024], replicated, may hold values from 0.5 to 1.5
- query_weight: bfloat16 [1024, 512], P(('dp', 'context'), 'tensor'), may hold values from -0.1875 to 0.1875
- key_weight: bfloat16 [1024, 512], P(('dp', 'context'), 'tensor'), may hold values from -0.1875 to 0.1875
- value_weight: bfloat16 [1024, 1024], P(('dp', 'context'), 'tensor'), may hold values from -0.1875 to 0.1875
- outgate_weight: bfloat16 [1024, 1024], P(('dp', 'context'), 'tensor'), may hold values from -0.1875 to 0.1875
- output_weight: bfloat16 [1024, 1024], P(('dp', 'context'), 'tensor'), may hold values from -0.375 to 0.375
- lowrank_weight: bfloat16 [1024, 16], replicated, may hold values from -0.1875 to 0.1875
- rankup_weight: bfloat16 [16, 512], P(None, 'tensor'), may hold values from -1.5 to 1.5
- gate_bias: float32 [512], P('tensor'), may hold values from 0.5 to 8
- head_gain: float32 [256], replicated, may hold values from 0.5 to 1.5
- norm_two: float32 [1024], replicated, may hold values from 0.5 to 1.5
- gate_weight: bfloat16 [1024, 2816], P(('dp', 'context'), 'tensor'), may hold values from -0.1875 to 0.1875
- up_weight: bfloat16 [1024, 2816], P(('dp', 'context'), 'tensor'), may hold values from -0.1875 to 0.1875
- down_weight: bfloat16 [1024, 2816], P(('dp', 'context'), 'tensor'), may hold values from -0.21875 to 0.21875
Outputs:
- outputs: bfloat16 [3072, 1024], P(('dp', 'context'))
- grad_inputs: float32 [3072, 1024], P(('dp', 'context'))
- grad_norm_one: float32 [1024], replicated
- grad_query: float32 [1024, 512], P(('dp', 'context'), 'tensor')
- grad_key: float32 [1024, 512], P(('dp', 'context'), 'tensor')
- grad_value: float32 [1024, 1024], P(('dp', 'context'), 'tensor')
- grad_outgate: float32 [1024, 1024], P(('dp', 'context'), 'tensor')
- grad_output: float32 [1024, 1024], P(('dp', 'context'), 'tensor')
- grad_lowrank: float32 [1024, 16], replicated
- grad_rankup: float32 [16, 512], P(None, 'tensor')
- grad_bias: float32 [512], P('tensor')
- grad_head_gain: float32 [256], replicated
- grad_norm_two: float32 [1024], replicated
- grad_gate: float32 [1024, 2816], P(('dp', 'context'), 'tensor')
- grad_up: float32 [1024, 2816], P(('dp', 'context'), 'tensor')
- grad_down: float32 [1024, 2816], P(('dp', 'context'), 'tensor')
All inputs are finite; a program needn't handle non-finite values.
Results may differ from a plain program's by a relative error of at most 0.011.
The roundings to bfloat16 on the way count: a program that leaves them out, or rounds other values in their place, can miss the bound.
Values may be sent and summed in bfloat16 or wider, within the bound.
No kernel may reach another device: no remote copies, remote signals or barrier semaphores. Data moves between devices by JAX's collectives and lax.ppermute only.
A program may use at most 128 MiB of HBM per device.

v0:
```python
import jax
import jax.numpy as jnp
from jax import lax
from jax.sharding import PartitionSpec as P

DK = 512
RANK = 16
GROUP = 64
HEAD_K = 128
HEAD_V = 256
highest_precision = lax.Precision.HIGHEST
epsilon = 1e-06


def carried_in(value, axis, join, neutral, backward):
    count, mine = (lax.axis_size(axis), lax.axis_index(axis))
    pieces = jax.tree.map(lambda part: lax.all_gather(part, axis), value)
    if backward:
        pieces = jax.tree.map(lambda part: part[::-1], pieces)
        mine = count - 1 - mine
    so_far = jax.tree.map(
        lambda part, zero: jnp.full_like(part, 0) + jnp.asarray(zero, part.dtype), value, neutral
    )

    def step(position, so_far):
        longer = join(so_far, jax.tree.map(lambda part: part[position], pieces))
        return jax.tree.map(lambda new, old: jnp.where(position < mine, new, old), longer, so_far)

    return lax.fori_loop(0, count - 1, step, so_far)


def rms_scale(vectors, gain):
    inverse = lax.rsqrt(jnp.mean(vectors * vectors, axis=-1, keepdims=True) + epsilon)
    return vectors * inverse * gain


def rms_back(vectors, gain, upstream):
    inverse = lax.rsqrt(jnp.mean(vectors * vectors, axis=-1, keepdims=True) + epsilon)
    normal_part = vectors * inverse
    scaled_up = upstream * gain
    back_vectors = inverse * (
        scaled_up - normal_part * jnp.mean(scaled_up * normal_part, axis=-1, keepdims=True)
    )
    return (back_vectors, upstream * normal_part)


def project(left, weight):
    return jnp.dot(left, weight, preferred_element_type=jnp.float32)


def project_back(left, weight):
    return lax.dot_general(
        left, weight, (((1,), (1,)), ((), ())), preferred_element_type=jnp.float32
    )


def weight_grad(left, right):
    return lax.dot_general(
        left, right, (((0,), (0,)), ((), ())), preferred_element_type=jnp.float32
    )


def swish_slope(preact):
    sigma = jax.nn.sigmoid(preact)
    return sigma * (1.0 + preact * (1.0 - sigma))


def gla_core(query, keys, values, log_decay):
    length = keys.shape[0]
    blocks = length // GROUP
    causal = jnp.tril(jnp.ones((GROUP, GROUP), jnp.float32))

    def advance(state, pieces):
        query_blk, key_blk, value_blk, decay_blk = pieces
        running = jnp.cumsum(decay_blk, axis=0)
        ending = running[-1]
        query_up = query_blk * jnp.exp(running)
        key_down = key_blk * jnp.exp(-running)
        scores = jnp.dot(query_up, key_down.T, precision=highest_precision) * causal
        within = jnp.dot(scores, value_blk, precision=highest_precision) + jnp.dot(
            query_up, state, precision=highest_precision
        )
        key_tail = key_blk * jnp.exp(ending - running)
        state = jnp.exp(ending)[:, None] * state + jnp.dot(
            key_tail.T, value_blk, precision=highest_precision
        )
        return (state, within)

    start_state = jnp.zeros((keys.shape[1], values.shape[1]), jnp.float32)
    final_state, pieces_out = lax.scan(
        advance,
        start_state,
        (
            query.reshape(blocks, GROUP, -1),
            keys.reshape(blocks, GROUP, -1),
            values.reshape(blocks, GROUP, -1),
            log_decay.reshape(blocks, GROUP, -1),
        ),
    )
    return (pieces_out.reshape(length, values.shape[1]), final_state)


def core_heads(query, keys, values, log_decay):
    return jax.vmap(gla_core, in_axes=(1, 1, 1, 1), out_axes=(1, 0))(query, keys, values, log_decay)


def gate_norm(attention_result, outgate, head_gain):
    return rms_scale(attention_result, head_gain) * outgate * jax.nn.sigmoid(outgate)


def span_result(query, keys, values, log_decay, incoming_state):
    local_output, local_state = core_heads(query, keys, values, log_decay)
    running = jnp.cumsum(log_decay, axis=0)
    decayed_state = query * jnp.exp(running)
    carried_state = jnp.einsum(
        "xbd,bdy->xby", decayed_state, incoming_state, precision=highest_precision
    )
    outgoing = jnp.exp(running[-1])[:, :, None] * incoming_state + local_state
    return (local_output + carried_state, outgoing)


def chain_combine(earlier, later):
    return (earlier[0] * later[0], later[0][:, :, None] * earlier[1] + later[1])


def local(
    inputs,
    cotangent,
    initial_state,
    norm_one,
    query_weight,
    key_weight,
    value_weight,
    outgate_weight,
    output_weight,
    lowrank_weight,
    rankup_weight,
    gate_bias,
    head_gain,
    norm_two,
    gate_weight,
    up_weight,
    down_weight,
):
    fetched = (
        lax.all_gather(query_weight, ("dp", "context"), axis=0, tiled=True),
        lax.all_gather(key_weight, ("dp", "context"), axis=0, tiled=True),
        lax.all_gather(value_weight, ("dp", "context"), axis=0, tiled=True),
        lax.all_gather(outgate_weight, ("dp", "context"), axis=0, tiled=True),
        lax.all_gather(output_weight, ("dp", "context"), axis=0, tiled=True),
        lax.all_gather(gate_weight, ("dp", "context"), axis=0, tiled=True),
        lax.all_gather(up_weight, ("dp", "context"), axis=0, tiled=True),
        lax.all_gather(down_weight, ("dp", "context"), axis=0, tiled=True),
    )
    rows = inputs.shape[0]
    heads_here = fetched[0].shape[1] // HEAD_K
    scale = HEAD_K ** (-0.5)
    stream = inputs.astype(jnp.float32)
    normed_one = rms_scale(stream, norm_one).astype(jnp.bfloat16)
    query = (project(normed_one, fetched[0]) * scale).reshape(rows, heads_here, HEAD_K)
    keys = project(normed_one, fetched[1]).reshape(rows, heads_here, HEAD_K)
    values = project(normed_one, fetched[2]).reshape(rows, heads_here, HEAD_V)
    outgate = project(normed_one, fetched[3]).reshape(rows, heads_here, HEAD_V)
    lowrank = project(normed_one, lowrank_weight).astype(jnp.bfloat16)
    gate_logit = project(lowrank, rankup_weight) + gate_bias
    log_decay = (jax.nn.log_sigmoid(gate_logit) / 16.0).reshape(rows, heads_here, HEAD_K)
    local_output, local_state = core_heads(query, keys, values, log_decay)
    running = jnp.cumsum(log_decay, axis=0)
    decay_total = jnp.exp(running[-1])
    decayed_state = query * jnp.exp(running)
    prefix = carried_in(
        (decay_total, local_state),
        "context",
        chain_combine,
        (jnp.ones_like(decay_total), jnp.zeros_like(local_state)),
        False,
    )
    incoming_state = prefix[0][:, :, None] * initial_state[0] + prefix[1]
    attention_result = local_output + jnp.einsum(
        "xbd,bdy->xby", decayed_state, incoming_state, precision=highest_precision
    )
    gated = gate_norm(attention_result, outgate, head_gain).reshape(rows, -1).astype(jnp.bfloat16)
    hidden = stream + lax.psum(project_back(gated, fetched[4]), "tensor")
    normed_two = rms_scale(hidden, norm_two).astype(jnp.bfloat16)
    gate_input = project(normed_two, fetched[5])
    up_input = project(normed_two, fetched[6])
    product = (jax.nn.silu(gate_input) * up_input).astype(jnp.bfloat16)
    result = hidden + lax.psum(project_back(product, fetched[7]), "tensor")
    weights = (
        lax.all_gather(query_weight, ("dp", "context"), axis=0, tiled=True),
        lax.all_gather(key_weight, ("dp", "context"), axis=0, tiled=True),
        lax.all_gather(value_weight, ("dp", "context"), axis=0, tiled=True),
        lax.all_gather(outgate_weight, ("dp", "context"), axis=0, tiled=True),
        lax.all_gather(output_weight, ("dp", "context"), axis=0, tiled=True),
        lax.all_gather(gate_weight, ("dp", "context"), axis=0, tiled=True),
        lax.all_gather(up_weight, ("dp", "context"), axis=0, tiled=True),
        lax.all_gather(down_weight, ("dp", "context"), axis=0, tiled=True),
    )
    back_product = project(cotangent, weights[7])
    grad_down = weight_grad(cotangent, product)
    back_up = (back_product * jax.nn.silu(gate_input)).astype(jnp.bfloat16)
    back_gate = (back_product * up_input * swish_slope(gate_input)).astype(jnp.bfloat16)
    grad_gate = weight_grad(normed_two, back_gate)
    grad_up = weight_grad(normed_two, back_up)
    back_normed_two = lax.psum(
        project_back(back_gate, weights[5]) + project_back(back_up, weights[6]), "tensor"
    )
    back_hidden_norm, gain_two_rows = rms_back(hidden, norm_two, back_normed_two)
    back_hidden = cotangent.astype(jnp.float32) + back_hidden_norm
    back_low = back_hidden.astype(jnp.bfloat16)
    back_gated = project(back_low, weights[4])
    grad_output = weight_grad(back_low, gated)
    ignored, gate_pull = jax.vjp(gate_norm, attention_result, outgate, head_gain)
    attention_backward_pass, back_outgate, grad_head = gate_pull(
        back_gated.reshape(rows, heads_here, HEAD_V)
    )
    pending_state = jnp.einsum(
        "rjm,rjy->jmy", decayed_state, attention_backward_pass, precision=highest_precision
    )
    suffix = carried_in(
        (decay_total, pending_state),
        "context",
        chain_combine,
        (jnp.ones_like(decay_total), jnp.zeros_like(pending_state)),
        True,
    )
    ignored, span_pull = jax.vjp(span_result, query, keys, values, log_decay, incoming_state)
    back_query, back_keys, back_values, back_decay, back_incoming = span_pull(
        (attention_backward_pass, suffix[1])
    )
    low_query = (back_query.reshape(rows, -1) * scale).astype(jnp.bfloat16)
    low_keys = back_keys.reshape(rows, -1).astype(jnp.bfloat16)
    low_values = back_values.reshape(rows, -1).astype(jnp.bfloat16)
    low_outgate = back_outgate.reshape(rows, -1).astype(jnp.bfloat16)
    back_logit = back_decay.reshape(rows, -1) * jax.nn.sigmoid(-gate_logit) / 16.0
    grad_bias = jnp.sum(back_logit, axis=0)
    low_logit = back_logit.astype(jnp.bfloat16)
    grad_rankup = weight_grad(lowrank, low_logit)
    back_lowrank = jnp.einsum(
        "shk,rhk->shr",
        low_logit.reshape(rows, heads_here, HEAD_K),
        rankup_weight.reshape(RANK, heads_here, HEAD_K),
        preferred_element_type=jnp.float32,
    ).astype(jnp.bfloat16)
    grad_lowrank = jnp.einsum(
        "sd,shr->dr", normed_one, back_lowrank, preferred_element_type=jnp.float32
    )
    grad_query = weight_grad(normed_one, low_query)
    grad_key = weight_grad(normed_one, low_keys)
    grad_value = weight_grad(normed_one, low_values)
    grad_outgate = weight_grad(normed_one, low_outgate)
    partial_one = (
        project_back(low_query, weights[0])
        + project_back(low_keys, weights[1])
        + project_back(low_values, weights[2])
        + project_back(low_outgate, weights[3])
        + jnp.einsum("shr,dr->sd", back_lowrank, lowrank_weight, preferred_element_type=jnp.float32)
    )
    back_normed_one = lax.psum(partial_one, "tensor")
    back_stream, gain_one_rows = rms_back(stream, norm_one, back_normed_one)
    grad_inputs = back_hidden + back_stream
    quarter = rows // lax.axis_size("tensor")
    begin = lax.axis_index("tensor") * quarter
    gain_one_part = jnp.sum(lax.dynamic_slice_in_dim(gain_one_rows, begin, quarter, 0), axis=0)
    gain_two_part = jnp.sum(lax.dynamic_slice_in_dim(gain_two_rows, begin, quarter, 0), axis=0)
    columns = grad_rankup.shape[1]
    offset = lax.axis_index("tensor") * columns
    rank_full = lax.dynamic_update_slice(
        jnp.zeros((RANK, DK), jnp.float32), grad_rankup, (0, offset)
    )
    bias_full = lax.dynamic_update_slice(jnp.zeros((DK,), jnp.float32), grad_bias, (offset,))
    summed = lax.psum(
        (gain_one_part, gain_two_part, grad_head, grad_lowrank, rank_full, bias_full),
        ("dp", "context", "tensor"),
    )
    rankup_shard = lax.dynamic_slice(summed[4], (0, offset), (RANK, columns))
    bias_shard = lax.dynamic_slice(summed[5], (offset,), (columns,))
    shards = (
        lax.psum_scatter(grad_query, ("dp", "context"), scatter_dimension=0, tiled=True),
        lax.psum_scatter(grad_key, ("dp", "context"), scatter_dimension=0, tiled=True),
        lax.psum_scatter(grad_value, ("dp", "context"), scatter_dimension=0, tiled=True),
        lax.psum_scatter(grad_outgate, ("dp", "context"), scatter_dimension=0, tiled=True),
        lax.psum_scatter(grad_output, ("dp", "context"), scatter_dimension=0, tiled=True),
        lax.psum_scatter(grad_gate, ("dp", "context"), scatter_dimension=0, tiled=True),
        lax.psum_scatter(grad_up, ("dp", "context"), scatter_dimension=0, tiled=True),
        lax.psum_scatter(grad_down, ("dp", "context"), scatter_dimension=0, tiled=True),
    )
    return (
        result.astype(jnp.bfloat16),
        grad_inputs,
        summed[0],
        shards[0],
        shards[1],
        shards[2],
        shards[3],
        shards[4],
        summed[3],
        rankup_shard,
        bias_shard,
        summed[2],
        summed[1],
        shards[5],
        shards[6],
        shards[7],
    )


def solution(mesh):
    placed = (
        P(("dp", "context"), None),
        P(("dp", "context"), None),
        P("dp", "tensor", None, None),
        P(),
        P(("dp", "context"), "tensor"),
        P(("dp", "context"), "tensor"),
        P(("dp", "context"), "tensor"),
        P(("dp", "context"), "tensor"),
        P(("dp", "context"), "tensor"),
        P(),
        P(None, "tensor"),
        P("tensor"),
        P(),
        P(),
        P(("dp", "context"), "tensor"),
        P(("dp", "context"), "tensor"),
        P(("dp", "context"), "tensor"),
    )
    return jax.shard_map(
        local,
        mesh=mesh,
        in_specs=placed,
        out_specs=(
            P(("dp", "context"), None),
            P(("dp", "context"), None),
            P(),
            P(("dp", "context"), "tensor"),
            P(("dp", "context"), "tensor"),
            P(("dp", "context"), "tensor"),
            P(("dp", "context"), "tensor"),
            P(("dp", "context"), "tensor"),
            P(),
            P(None, "tensor"),
            P("tensor"),
            P(),
            P(),
            P(("dp", "context"), "tensor"),
            P(("dp", "context"), "tensor"),
            P(("dp", "context"), "tensor"),
        ),
        check_vma=False,
    )
```

profile of v0, /device:TPU:0, one launch (start us, length us, event | category | flops | bytes accessed | tf_op | source)
XLA Modules:
  0.0 835.5 jit_solution(9248610303740419045)
XLA Ops:
  9.5 2.5 convert_multiply_fusion
  13.6 25.4 %all_gather.52 = bf16[1024,128]{1,0:T(8,128)(2,1)S(1)} all-gather(bf16[128,128]{1,0:T(8,128)(2,1)S(1)} %copy-done.48), channel_id=1, replica_groups=mesh['dp'=2,'context'=4,'tensor'=4] {'dp','context'}, dimensions={0}, use_global_device_ids=true | all-gather | bytes 294912 | tf_op jit(solution)/shard_map/all_gather | solution.py:146
  39.7 24.6 %all_gather.51 = bf16[1024,256]{1,0:T(8,128)(2,1)S(1)} all-gather(bf16[128,256]{1,0:T(8,128)(2,1)S(1)} %copy-done.41), channel_id=1, replica_groups=mesh['dp'=2,'context'=4,'tensor'=4] {'dp','context'}, dimensions={0}, use_global_device_ids=true | all-gather | bytes 589824 | tf_op jit(solution)/shard_map/all_gather | solution.py:148
  64.7 23.7 %all_gather.50 = bf16[1024,128]{1,0:T(8,128)(2,1)S(1)} all-gather(bf16[128,128]{1,0:T(8,128)(2,1)S(1)} %copy-done.49), channel_id=1, replica_groups=mesh['dp'=2,'context'=4,'tensor'=4] {'dp','context'}, dimensions={0}, use_global_device_ids=true | all-gather | bytes 294912 | tf_op jit(solution)/shard_map/all_gather | solution.py:147
  89.1 7.0 while.106
  96.8 10.7 %all-gather = f32[4,128,256]{2,1,0:T(8,128)S(1)} all-gather(f32[1,128,256]{2,1,0:T(8,128)S(1)} %get-tuple-element.770), channel_id=2, replica_groups=mesh['dp'=2,'context'=4,'tensor'=4] {'context'}, dimensions={0}, use_global_device_ids=true | all-gather | bytes 655360 | tf_op jit(solution)/shard_map/all_gather | solution.py:17
  108.2 7.2 all_gather.53
  117.0 24.7 %all_gather.56 = bf16[1024,256]{1,0:T(8,128)(2,1)S(1)} all-gather(bf16[128,256]{1,0:T(8,128)(2,1)S(1)} %copy-done.42), channel_id=1, replica_groups=mesh['dp'=2,'context'=4,'tensor'=4] {'dp','context'}, dimensions={0}, use_global_device_ids=true | all-gather | bytes 589824 | tf_op jit(solution)/shard_map/all_gather | solution.py:149
  142.2 24.6 %all_gather.57 = bf16[1024,256]{1,0:T(8,128)(2,1)S(1)} all-gather(bf16[128,256]{1,0:T(8,128)(2,1)S(1)} %copy-done.43), channel_id=1, replica_groups=mesh['dp'=2,'context'=4,'tensor'=4] {'dp','context'}, dimensions={0}, use_global_device_ids=true | all-gather | bytes 589824 | tf_op jit(solution)/shard_map/all_gather | solution.py:150
  171.8 67.8 %all-reduce.9.cloned.1.call-done = f32[384,1024]{1,0:T(8,128)} async-done(((f32[384,1024]{1,0:T(8,128)}), f32[384,1024]{1,0:T(8,128)}) %all-reduce.9.cloned.1.call-update) | async-done | bytes 1572880 | tf_op jit(solution)/shard_map/psum | solution.py:183
  242.6 4.2 fusion.171
  246.8 3.5 fusion.172
  251.6 4.4 multiply_convert_fusion.2
  262.8 53.0 %while.109 = (s32[]{:T(128)}, f32[1,128,256]{2,1,0:T(8,128)S(1)}, f32[6,1,64,128]{3,2,1,0:T(8,128)}, f32[6,1,64,128]{3,2,1,0:T(8,128)}, f32[6,1,128,64]{2,3,1,0:...) while((s32[]{:T(128)}, f32[1,128,256]{2,1,0:T(8,128)S(1)}, ...), condition=%wide.region_19.20_spmd.clone.clone, body=%wide.region_17.19_spmd.clone.sunk.clone | while | flops 32215044 | bytes 1288872 | solution.py:90
  317.8 3.5 fusion.173
  321.3 7.6 all-reduce.11.cloned.1.call-done
  336.5 10.7 %all-gather.1 = f32[512,256]{1,0:T(8,128)} all-gather(f32[128,256]{1,0:T(8,128)S(1)} %fusion.128), channel_id=3, replica_groups=mesh['dp'=2,'context'=4,'tensor'=4] {'context'}, dimensions={0}, use_global_device_ids=true | all-gather | bytes 655360 | tf_op jit(solution)/shard_map/all_gather | solution.py:17
  349.1 3.1 while.108
  356.8 2.5 fusion.125
  361.4 115.1 %while.105 = (s32[]{:T(128)}, f32[1,128,256]{1,2,0:T(8,128)S(1)}, f32[6,1,64,128]{3,2,1,0:T(8,128)}, bf16[6,1,64,128]{3,2,1,0:T(8,128)(2,1)}, bf16[6,1,64,256]{3...) while((s32[]{:T(128)}, f32[1,128,256]{1,2,0:T(8,128)S(1)}, ...), condition=%wide.region_24.25_spmd.clone.clone, body=%wide.region_20.24_spmd.clone.sunk.clone | while | flops 139243520 | bytes 3109597 | solution.py:90
  489.8 2.1 fusion.179
  492.0 2.4 fusion.180
  494.5 2.4 fusion.132
  499.9 3.5 fusion.182
  503.5 3.6 fusion.183
  508.2 3.6 convolution_bitcast_fusion.5
  513.5 92.7 %all-reduce.15.cloned.1.call-done = (f32[384,1024]{1,0:T(8,128)}, f32[384,1024]{1,0:T(8,128)}) async-done(((f32[384,1024]{1,0:T(8,128)}, f32[384,1024]{1,0:T(8,128)}), (f32[384,1024]{1,0:T(8,128)}, f32[384,1024]{1,0:T(8,128)})) %all-reduce.15.cloned.1.call-update) | async-done | bytes 3145744 | tf_op jit(solution)/shard_map/psum | solution.py:188
  607.4 40.1 %all-reduce.2 = (f32[1024]{0:T(1024)}, f32[16,512]{1,0:T(8,128)S(1)}, f32[512]{0:T(512)S(1)}, f32[256]{0:T(256)}, f32[1024]{0:T(1024)}) all-reduce(f32[1024]{0:T(1024)S(1)} %fusion.124, f32[16,512]{1,0:T(8,128)S(1)} %convolution_dynamic-update-slice_fusion, ...), channel_id=1, replica_groups=mesh['dp'=2,'context'=4,'tensor'=4] {'dp','context','tensor'}, use_global_device_ids=true, to_apply=%region_31.32 | all-reduce | flops 11008 | bytes 88064 | tf_op jit(solution)/shard_map/psum | solution.py:272
  650.5 3.9 multiply_add_fusion
  654.5 79.4 %all-reduce.13.cloned.1.call-done = f32[1024,16]{0,1:T(8,128)} async-done(((f32[1024,16]{0,1:T(8,128)}), f32[1024,16]{0,1:T(8,128)}) %all-reduce.13.cloned.1.call-update) | async-done | bytes 65552 | tf_op jit(solution)/shard_map/psum | solution.py:272
  733.9 44.3 %reduce-scatter.21.cloned.1.call-done = f32[128,704]{0,1:T(8,128)} async-done(((f32[1024,704]{0,1:T(8,128)}), f32[128,704]{0,1:T(8,128)}) %reduce-scatter.21.cloned.1.call-update) | async-done | bytes 360464 | tf_op jit(solution)/shard_map/reduce_scatter | solution.py:285
  778.2 48.4 %reduce-scatter.23.cloned.1.call-done = f32[128,704]{0,1:T(8,128)} async-done(((f32[1024,704]{0,1:T(8,128)}), f32[128,704]{0,1:T(8,128)}) %reduce-scatter.23.cloned.1.call-update) | async-done | bytes 360464 | tf_op jit(solution)/shard_map/reduce_scatter | solution.py:286
  (471 shorter events, 244.5 us)
Async XLA Ops:
  8.0 231.5 %all-reduce.9.cloned.1.call-start = ((), (), s32[]{:S(2)}) async-start(), calls=%async_computation.8 | async-start | bytes 3145728 | tf_op jit(solution)/shard_map/psum | solution.py:183
  12.4 27.3 %copy-start.41 = (bf16[128,256]{1,0:T(8,128)(2,1)S(1)}, bf16[128,256]{1,0:T(8,128)(2,1)}, u32[]{:S(2)}) copy-start(bf16[128,256]{1,0:T(8,128)(2,1)} %param.33) | copy-start | bytes 196612
  13.5 94.0 %copy-start.29 = (f32[128,1,3,128]{0,3,2,1:T(8,128)}, f32[128,1,3,128]{0,3,2,1:T(8,128)S(1)}, u32[]{:S(2)}) copy-start(f32[128,1,3,128]{0,3,2,1:T(8,128)S(1)} %copy.99) | copy-start | bytes 589828
  39.0 25.7 %copy-start.49 = (bf16[128,128]{1,0:T(8,128)(2,1)S(1)}, bf16[128,128]{1,0:T(8,128)(2,1)}, u32[]{:S(2)}) copy-start(bf16[128,128]{1,0:T(8,128)(2,1)} %param.32) | copy-start | bytes 98308
  64.3 24.5 %copy-start.15 = (bf16[1024,256]{1,0:T(8,128)(2,1)}, bf16[1024,256]{1,0:T(8,128)(2,1)S(1)}, u32[]{:S(2)}) copy-start(bf16[1024,256]{1,0:T(8,128)(2,1)S(1)} %all_gather.51) | copy-start | bytes 1572868
  96.8 18.7 %copy-start.6 = (f32[6,1,64,128]{3,2,1,0:T(8,128)}, f32[6,1,64,128]{3,2,1,0:T(8,128)S(1)}, u32[]{:S(2)}) copy-start(f32[6,1,64,128]{3,2,1,0:T(8,128)S(1)} %get-tuple-element.1963) | copy-start | bytes 589828
  115.9 26.3 %copy-start.50 = (f32[4,1,128]{2,1,0:T(1,128)}, f32[4,1,128]{2,1,0:T(1,128)S(1)}, u32[]{:S(2)}) copy-start(f32[4,1,128]{2,1,0:T(1,128)S(1)} %get-tuple-element.1997) | copy-start | bytes 6148
  116.2 25.9 %copy-start.43 = (bf16[128,256]{1,0:T(8,128)(2,1)S(1)}, bf16[128,256]{1,0:T(8,128)(2,1)}, u32[]{:S(2)}) copy-start(bf16[128,256]{1,0:T(8,128)(2,1)} %param.35) | copy-start | bytes 196612
  116.9 50.0 %copy-start.11 = (f32[384,1,256]{0,2,1:T(8,128)}, f32[384,1,256]{0,2,1:T(8,128)S(1)}, u32[]{:S(2)}) copy-start(f32[384,1,256]{0,2,1:T(8,128)S(1)} %get-tuple-element.1254) | copy-start | bytes 1179652
  116.9 50.0 %copy-start.53 = (f32[384]{0:T(512)}, f32[384]{0:T(512)S(1)}, u32[]{:S(2)}) copy-start(f32[384]{0:T(512)S(1)} %get-tuple-element.1253) | copy-start | bytes 4612
  116.9 49.8 %copy-start.55 = (f32[256]{0:T(256)S(1)}, f32[256]{0:T(256)}, u32[]{:S(2)}) copy-start(f32[256]{0:T(256)} %param.39) | copy-start | bytes 3076
  141.7 25.3 %copy-start.17 = (bf16[1024,256]{1,0:T(8,128)(2,1)}, bf16[1024,256]{1,0:T(8,128)(2,1)S(1)}, u32[]{:S(2)}) copy-start(bf16[1024,256]{1,0:T(8,128)(2,1)S(1)} %all_gather.56) | copy-start | bytes 1572868
  142.2 24.8 %copy-start.13 = (f32[384,256]{0,1:T(8,128)}, f32[384,256]{0,1:T(8,128)S(1)}, u32[]{:S(2)}) copy-start(f32[384,256]{0,1:T(8,128)S(1)} %fusion.169) | copy-start | bytes 1179652
  169.9 69.7 %copy-start.1 = (bf16[384,1024]{1,0:T(8,128)(2,1)S(1)}, bf16[384,1024]{1,0:T(8,128)(2,1)}, u32[]{:S(2)}) copy-start(bf16[384,1024]{1,0:T(8,128)(2,1)} %param.27) | copy-start | bytes 2359300
  169.9 71.5 %copy-start.47 = (f32[1024]{0:T(1024)S(1)}, f32[1024]{0:T(1024)}, u32[]{:S(2)}) copy-start(f32[1024]{0:T(1024)} %param.40) | copy-start | bytes 12292
  169.9 72.7 %all-gather.6.cloned.1.call-start = ((), (), s32[]{:S(2)}) async-start(), calls=%async_computation.9 | async-start | bytes 1622016 | tf_op jit(solution)/shard_map/all_gather | solution.py:151
  170.5 76.3 %all-gather.8.cloned.1.call-start = ((), (), s32[]{:S(2)}) async-start(), calls=%async_computation.10 | async-start | bytes 1622016 | tf_op jit(solution)/shard_map/all_gather | solution.py:152
  171.1 80.5 %all-gather.10.cloned.1.call-start = ((), (), s32[]{:S(2)}) async-start(), calls=%async_computation.11 | async-start | bytes 1622016 | tf_op jit(solution)/shard_map/all_gather | solution.py:153
  171.7 157.3 %all-reduce.11.cloned.1.call-start = ((), (), s32[]{:S(2)}) async-start(), calls=%async_computation.12 | async-start | bytes 3145728 | tf_op jit(solution)/shard_map/psum | solution.py:205
  242.6 86.3 %copy-start.2 = (f32[384,1024]{1,0:T(8,128)}, f32[384,1024]{1,0:T(8,128)S(1)}, u32[]{:S(2)}) copy-start(f32[384,1024]{1,0:T(8,128)S(1)} %get-tuple-element.1225) | copy-start | bytes 4718596
  259.8 346.4 %all-reduce.15.cloned.1.call-start = ((), (), s32[]{:S(2)}) async-start(), calls=%async_computation.22 | async-start | bytes 6291456 | tf_op jit(solution)/shard_map/psum | solution.py:188
  486.7 247.2 %all-reduce.13.cloned.1.call-start = ((), (), s32[]{:S(2)}) async-start(), calls=%async_computation.18 | async-start | bytes 131072 | tf_op jit(solution)/shard_map/psum | solution.py:272
  487.6 246.3 %reduce-scatter.9.cloned.1.call-start = ((), (), s32[]{:S(2)}) async-start(), calls=%async_computation.13 | async-start | bytes 589824 | tf_op jit(solution)/shard_map/reduce_scatter | solution.py:279
  489.8 244.1 %reduce-scatter.11.cloned.1.call-start = ((), (), s32[]{:S(2)}) async-start(), calls=%async_computation.14 | async-start | bytes 589824 | tf_op jit(solution)/shard_map/reduce_scatter | solution.py:280
  492.0 241.9 %reduce-scatter.13.cloned.1.call-start = ((), (), s32[]{:S(2)}) async-start(), calls=%async_computation.15 | async-start | bytes 1179648 | tf_op jit(solution)/shard_map/reduce_scatter | solution.py:281
  494.5 239.4 %reduce-scatter.17.cloned.1.call-start = ((), (), s32[]{:S(2)}) async-start(), calls=%async_computation.17 | async-start | bytes 1179648 | tf_op jit(solution)/shard_map/reduce_scatter | solution.py:283
  497.0 236.9 %reduce-scatter.15.cloned.1.call-start = ((), (), s32[]{:S(2)}) async-start(), calls=%async_computation.16 | async-start | bytes 1179648 | tf_op jit(solution)/shard_map/reduce_scatter | solution.py:282
  498.8 235.2 %reduce-scatter.19.cloned.1.call-start = ((), (), s32[]{:S(2)}) async-start(), calls=%async_computation.19 | async-start | bytes 3244032 | tf_op jit(solution)/shard_map/reduce_scatter | solution.py:284
  503.5 274.8 %reduce-scatter.21.cloned.1.call-start = ((), (), s32[]{:S(2)}) async-start(), calls=%async_computation.20 | async-start | bytes 3244032 | tf_op jit(solution)/shard_map/reduce_scatter | solution.py:285
  507.1 319.5 %reduce-scatter.23.cloned.1.call-start = ((), (), s32[]{:S(2)}) async-start(), calls=%async_computation.21 | async-start | bytes 3244032 | tf_op jit(solution)/shard_map/reduce_scatter | solution.py:286
  511.9 95.5 %copy-start.57 = (f32[256]{0:T(256)S(1)}, f32[256]{0:T(256)}, u32[]{:S(2)}) copy-start(f32[256]{0:T(256)} %get-tuple-element.1105) | copy-start | bytes 3076
  511.9 136.8 %copy-start.46 = (f32[1024]{0:T(1024)S(1)}, f32[1024]{0:T(1024)}, u32[]{:S(2)}) copy-start(f32[1024]{0:T(1024)} %param.30) | copy-start | bytes 12292
  (45 other events, 109.2 us)
Sparse Core Ops, SparseCore 0:
  170.0 69.4 all-reduce.8
  259.9 68.9 all-reduce.10
  486.8 119.3 all-reduce.14
  612.3 121.5 all-reduce.12
Sparse Core Ops, SparseCore 1:
  172.3 25.6 all-gather.5
  199.7 25.0 all-gather.7
  226.5 25.0 all-gather.9
  492.0 32.4 reduce-scatter.8
  528.2 34.1 reduce-scatter.10
  566.1 35.9 reduce-scatter.12
  605.7 35.9 reduce-scatter.16
  645.2 35.9 reduce-scatter.14
  685.1 44.6 reduce-scatter.18
  733.7 44.5 reduce-scatter.20
  782.1 44.5 reduce-scatter.22
where the time goes:
time: 843 us; the launch traced here: 835 us
  waiting for transfers between devices  343 us (41%)
  blocking collectives  192 us (23%)
  matrix products  140 us (17%)
  other arithmetic  77.7 us (9%)
  local copies, waits for them, and re-layouts  64.1 us (8%)
  between operations  16.4 us (2%)
    psum x1, waiting for transfers between devices, local(): result = hidden + lax.psum(project_back(product, fetched[7]), 'tensor')  92.7 us
    psum x1, waiting for transfers between devices, local(): lax.psum((gain_one_part, gain_two_part, grad_head, grad_lowrank, rank_ful...  79.4 us
    psum x1, waiting for transfers between devices, local(): hidden = stream + lax.psum(project_back(gated, fetched[4]), 'tensor')  67.8 us
    reduce_scatter x1, waiting for transfers between devices, local(): lax.psum_scatter(grad_down, ('dp', 'context'), scatter_dimension=0, tiled...  48.4 us
    reduce_scatter x1, waiting for transfers between devices, local(): lax.psum_scatter(grad_up, ('dp', 'context'), scatter_dimension=0, tiled=T...  44.3 us
    psum x1, blocking collectives, local(): lax.psum((gain_one_part, gain_two_part, grad_head, grad_lowrank, rank_ful...  40.1 us
    dot_general x24, matrix products, advance(): scores = jnp.dot(query_up, key_down.T, precision=highest_precision) * causal  29.7 us
    all_gather x3, blocking collectives, carried_in(): pieces = jax.tree.map(lambda part: lax.all_gather(part, axis), value)  28.6 us
  transfers between devices with their start and end apart: 15, of which 7 were waited for; matrix products, arithmetic and copies ran while one was open for 12% of the time, Pallas kernels for 0%

commit v1 on v0

--- a/solution.py
+++ b/solution.py
@@ -269,10 +269,9 @@
         jnp.zeros((RANK, DK), jnp.float32), grad_rankup, (0, offset)
     )
     bias_full = lax.dynamic_update_slice(jnp.zeros((DK,), jnp.float32), grad_bias, (offset,))
-    summed = lax.psum(
-        (gain_one_part, gain_two_part, grad_head, grad_lowrank, rank_full, bias_full),
-        ("dp", "context", "tensor"),
-    )
+    summed = (gain_one_part, gain_two_part, grad_head, grad_lowrank, rank_full, bias_full)
+    for mesh_axis in ("dp", ("context", "tensor")):
+        summed = lax.psum(summed, mesh_axis)
     rankup_shard = lax.dynamic_slice(summed[4], (0, offset), (RANK, columns))
     bias_shard = lax.dynamic_slice(summed[5], (offset,), (columns,))
     shards = (

time: 843 us -> 864 us (1.025)
  blocking collectives: 192 us -> 231 us
  waiting for transfers between devices: 343 us -> 318 us
    psum x1 -> x2, waiting for transfers between devices: 79.4 us -> 35.1 us  [local(): summed = lax.psum(summed, mesh_axis)]
    psum x1 -> x2, blocking collectives: 40.1 us -> 79.7 us  [local(): summed = lax.psum(summed, mesh_axis)]
    reduce_scatter x1, waiting for transfers between devices: 0.02 us -> 8.8 us  [local(): lax.psum_scatter(grad_gate, ('dp', 'context'), scatter_dimension=0, tiled...]
  transfers between devices with their start and end apart: 15 -> 16, of which waited for: 7 -> 9; matrix products, arithmetic and copies ran while one was open for 12% -> 13% of each run, Pallas kernels for 0% -> 0%
where the time goes in v1:
time: 864 us; the launch traced here: 857 us
  waiting for transfers between devices  318 us (37%)
  blocking collectives  231 us (27%)
  matrix products  148 us (17%)
  other arithmetic  78.1 us (9%)
  local copies, waits for them, and re-layouts  63.5 us (7%)
  between operations  16.4 us (2%)
    psum x1, waiting for transfers between devices, local(): result = hidden + lax.psum(project_back(product, fetched[7]), 'tensor')  98.8 us
    psum x2, blocking collectives, local(): summed = lax.psum(summed, mesh_axis)  79.7 us
    psum x1, waiting for transfers between devices, local(): hidden = stream + lax.psum(project_back(gated, fetched[4]), 'tensor')  67.7 us
    reduce_scatter x1, waiting for transfers between devices, local(): lax.psum_scatter(grad_up, ('dp', 'context'), scatter_dimension=0, tiled=T...  48.6 us
    reduce_scatter x1, waiting for transfers between devices, local(): lax.psum_scatter(grad_down, ('dp', 'context'), scatter_dimension=0, tiled...  48.4 us
    psum x2, waiting for transfers between devices, local(): summed = lax.psum(summed, mesh_axis)  35.1 us
    dot_general x24, matrix products, advance(): scores = jnp.dot(query_up, key_down.T, precision=highest_precision) * causal  29.7 us
    all_gather x3, blocking collectives, carried_in(): pieces = jax.tree.map(lambda part: lax.all_gather(part, axis), value)  28.7 us
  transfers between devices with their start and end apart: 16, of which 9 were waited for; matrix products, arithmetic and copies ran while one was open for 13% of the time, Pallas kernels for 0%

profile of v1, /device:TPU:0, one launch (start us, length us, event | category | flops | bytes accessed | tf_op | source)
XLA Modules:
  0.0 856.9 jit_solution(4906647837908122816)
XLA Ops:
  13.6 25.4 %all_gather.52 = bf16[1024,128]{1,0:T(8,128)(2,1)S(1)} all-gather(bf16[128,128]{1,0:T(8,128)(2,1)S(1)} %copy-done.48), channel_id=1, replica_groups=mesh['dp'=2,'context'=4,'tensor'=4] {'dp','context'}, dimensions={0}, use_global_device_ids=true | all-gather | bytes 294912 | tf_op jit(solution)/shard_map/all_gather | solution.py:146
  39.7 24.6 %all_gather.51 = bf16[1024,256]{1,0:T(8,128)(2,1)S(1)} all-gather(bf16[128,256]{1,0:T(8,128)(2,1)S(1)} %copy-done.41), channel_id=1, replica_groups=mesh['dp'=2,'context'=4,'tensor'=4] {'dp','context'}, dimensions={0}, use_global_device_ids=true | all-gather | bytes 589824 | tf_op jit(solution)/shard_map/all_gather | solution.py:148
  64.7 23.7 %all_gather.50 = bf16[1024,128]{1,0:T(8,128)(2,1)S(1)} all-gather(bf16[128,128]{1,0:T(8,128)(2,1)S(1)} %copy-done.49), channel_id=1, replica_groups=mesh['dp'=2,'context'=4,'tensor'=4] {'dp','context'}, dimensions={0}, use_global_device_ids=true | all-gather | bytes 294912 | tf_op jit(solution)/shard_map/all_gather | solution.py:147
  89.1 7.0 while.106
  96.8 10.7 %all-gather = f32[4,128,256]{2,1,0:T(8,128)S(1)} all-gather(f32[1,128,256]{2,1,0:T(8,128)S(1)} %get-tuple-element.770), channel_id=2, replica_groups=mesh['dp'=2,'context'=4,'tensor'=4] {'context'}, dimensions={0}, use_global_device_ids=true | all-gather | bytes 655360 | tf_op jit(solution)/shard_map/all_gather | solution.py:17
  108.3 7.2 all_gather.53
  117.0 24.7 %all_gather.56 = bf16[1024,256]{1,0:T(8,128)(2,1)S(1)} all-gather(bf16[128,256]{1,0:T(8,128)(2,1)S(1)} %copy-done.42), channel_id=1, replica_groups=mesh['dp'=2,'context'=4,'tensor'=4] {'dp','context'}, dimensions={0}, use_global_device_ids=true | all-gather | bytes 589824 | tf_op jit(solution)/shard_map/all_gather | solution.py:149
  142.2 24.5 %all_gather.57 = bf16[1024,256]{1,0:T(8,128)(2,1)S(1)} all-gather(bf16[128,256]{1,0:T(8,128)(2,1)S(1)} %copy-done.43), channel_id=1, replica_groups=mesh['dp'=2,'context'=4,'tensor'=4] {'dp','context'}, dimensions={0}, use_global_device_ids=true | all-gather | bytes 589824 | tf_op jit(solution)/shard_map/all_gather | solution.py:150
  171.8 67.7 %all-reduce.11.cloned.1.call-done = f32[384,1024]{1,0:T(8,128)} async-done(((f32[384,1024]{1,0:T(8,128)}), f32[384,1024]{1,0:T(8,128)}) %all-reduce.11.cloned.1.call-update) | async-done | bytes 1572880 | tf_op jit(solution)/shard_map/psum | solution.py:183
  242.6 4.2 fusion.171
  246.8 3.5 fusion.172
  251.6 4.4 multiply_convert_fusion.2
  262.8 53.1 %while.109 = (s32[]{:T(128)}, f32[1,128,256]{2,1,0:T(8,128)S(1)}, f32[6,1,64,128]{3,2,1,0:T(8,128)}, f32[6,1,64,128]{3,2,1,0:T(8,128)}, f32[6,1,128,64]{2,3,1,0:...) while((s32[]{:T(128)}, f32[1,128,256]{2,1,0:T(8,128)S(1)}, ...), condition=%wide.region_19.20_spmd.clone.clone, body=%wide.region_17.19_spmd.clone.sunk.clone | while | flops 32215044 | bytes 1288872 | solution.py:90
  317.9 3.5 fusion.173
  321.4 7.5 all-reduce.13.cloned.1.call-done
  336.5 10.7 %all-gather.1 = f32[512,256]{1,0:T(8,128)} all-gather(f32[128,256]{1,0:T(8,128)S(1)} %fusion.128), channel_id=3, replica_groups=mesh['dp'=2,'context'=4,'tensor'=4] {'context'}, dimensions={0}, use_global_device_ids=true | all-gather | bytes 655360 | tf_op jit(solution)/shard_map/all_gather | solution.py:17
  349.1 3.1 while.108
  361.3 115.2 %while.105 = (s32[]{:T(128)}, f32[1,128,256]{1,2,0:T(8,128)S(1)}, f32[6,1,64,128]{3,2,1,0:T(8,128)}, bf16[6,1,64,128]{3,2,1,0:T(8,128)(2,1)}, bf16[6,1,64,256]{3...) while((s32[]{:T(128)}, f32[1,128,256]{1,2,0:T(8,128)S(1)}, ...), condition=%wide.region_24.25_spmd.clone.clone, body=%wide.region_20.24_spmd.clone.sunk.clone | while | flops 139243520 | bytes 3109597 | solution.py:90
  481.8 2.6 fusion.175
  490.0 4.4 add_add_fusion
  494.5 11.6 %all-reduce.15.cloned.1.call-done = f32[1024,16]{0,1:T(8,128)} async-done(((f32[1024,16]{0,1:T(8,128)}), f32[1024,16]{0,1:T(8,128)}) %all-reduce.15.cloned.1.call-update) | async-done | bytes 65552 | tf_op jit(solution)/shard_map/psum | solution.py:274
  518.3 3.5 fusion.182
  521.9 3.6 fusion.183
  526.7 3.6 convolution_bitcast_fusion.5
  531.9 98.8 %all-reduce.19.cloned.1.call-done = (f32[384,1024]{1,0:T(8,128)}, f32[384,1024]{1,0:T(8,128)}) async-done(((f32[384,1024]{1,0:T(8,128)}, f32[384,1024]{1,0:T(8,128)}), (f32[384,1024]{1,0:T(8,128)}, f32[384,1024]{1,0:T(8,128)})) %all-reduce.19.cloned.1.call-update) | async-done | bytes 3145744 | tf_op jit(solution)/shard_map/psum | solution.py:188
  631.9 3.5 all-reduce.4
  635.4 76.1 %all-reduce.2 = (f32[1024]{0:T(1024)}, f32[16,512]{1,0:T(8,128)S(1)}, f32[512]{0:T(512)S(1)}, f32[256]{0:T(256)}, f32[1024]{0:T(1024)}) all-reduce(f32[1024]{0:T(1024)S(1)} %get-tuple-element.1222, f32[16,512]{1,0:T(8,128)S(1)} %get-tuple-element.1223, ...), channel_id=1, replica_groups=mesh['dp'=2,'context'=4,'tensor'=4] {'context','tensor'}, use_global_device_ids=true, to_apply=%region_32.33 | all-reduce | flops 11008 | bytes 88064 | tf_op jit(solution)/shard_map/psum | solution.py:274
  714.7 4.1 multiply_add_fusion
  718.8 23.5 %all-reduce.17.cloned.1.call-done = f32[1024,16]{0,1:T(8,128)} async-done(((f32[1024,16]{0,1:T(8,128)}), f32[1024,16]{0,1:T(8,128)}) %all-reduce.17.cloned.1.call-update) | async-done | bytes 65552 | tf_op jit(solution)/shard_map/psum | solution.py:274
  742.3 8.8 %reduce-scatter.19.cloned.1.call-done = f32[128,704]{0,1:T(8,128)} async-done(((f32[1024,704]{0,1:T(8,128)}), f32[128,704]{0,1:T(8,128)}) %reduce-scatter.19.cloned.1.call-update) | async-done | bytes 360464 | tf_op jit(solution)/shard_map/reduce_scatter | solution.py:283
  751.1 48.6 %reduce-scatter.21.cloned.1.call-done = f32[128,704]{0,1:T(8,128)} async-done(((f32[1024,704]{0,1:T(8,128)}), f32[128,704]{0,1:T(8,128)}) %reduce-scatter.21.cloned.1.call-update) | async-done | bytes 360464 | tf_op jit(solution)/shard_map/reduce_scatter | solution.py:284
  799.7 48.4 %reduce-scatter.23.cloned.1.call-done = f32[128,704]{0,1:T(8,128)} async-done(((f32[1024,704]{0,1:T(8,128)}), f32[128,704]{0,1:T(8,128)}) %reduce-scatter.23.cloned.1.call-update) | async-done | bytes 360464 | tf_op jit(solution)/shard_map/reduce_scatter | solution.py:285
  (475 shorter events, 256.6 us)
Async XLA Ops:
  8.0 231.5 %all-reduce.11.cloned.1.call-start = ((), (), s32[]{:S(2)}) async-start(), calls=%async_computation.8 | async-start | bytes 3145728 | tf_op jit(solution)/shard_map/psum | solution.py:183
  12.4 27.3 %copy-start.41 = (bf16[128,256]{1,0:T(8,128)(2,1)S(1)}, bf16[128,256]{1,0:T(8,128)(2,1)}, u32[]{:S(2)}) copy-start(bf16[128,256]{1,0:T(8,128)(2,1)} %param.33) | copy-start | bytes 196612
  13.5 94.1 %copy-start.29 = (f32[128,1,3,128]{0,3,2,1:T(8,128)}, f32[128,1,3,128]{0,3,2,1:T(8,128)S(1)}, u32[]{:S(2)}) copy-start(f32[128,1,3,128]{0,3,2,1:T(8,128)S(1)} %copy.99) | copy-start | bytes 589828
  39.0 25.7 %copy-start.49 = (bf16[128,128]{1,0:T(8,128)(2,1)S(1)}, bf16[128,128]{1,0:T(8,128)(2,1)}, u32[]{:S(2)}) copy-start(bf16[128,128]{1,0:T(8,128)(2,1)} %param.32) | copy-start | bytes 98308
  64.3 24.5 %copy-start.15 = (bf16[1024,256]{1,0:T(8,128)(2,1)}, bf16[1024,256]{1,0:T(8,128)(2,1)S(1)}, u32[]{:S(2)}) copy-start(bf16[1024,256]{1,0:T(8,128)(2,1)S(1)} %all_gather.51) | copy-start | bytes 1572868
  116.0 26.3 %copy-start.50 = (f32[4,1,128]{2,1,0:T(1,128)}, f32[4,1,128]{2,1,0:T(1,128)S(1)}, u32[]{:S(2)}) copy-start(f32[4,1,128]{2,1,0:T(1,128)S(1)} %get-tuple-element.2006) | copy-start | bytes 6148
  116.3 25.9 %copy-start.43 = (bf16[128,256]{1,0:T(8,128)(2,1)S(1)}, bf16[128,256]{1,0:T(8,128)(2,1)}, u32[]{:S(2)}) copy-start(bf16[128,256]{1,0:T(8,128)(2,1)} %param.35) | copy-start | bytes 196612
  117.0 50.0 %copy-start.11 = (f32[384,1,256]{0,2,1:T(8,128)}, f32[384,1,256]{0,2,1:T(8,128)S(1)}, u32[]{:S(2)}) copy-start(f32[384,1,256]{0,2,1:T(8,128)S(1)} %get-tuple-element.1259) | copy-start | bytes 1179652
  117.0 50.0 %copy-start.53 = (f32[384]{0:T(512)}, f32[384]{0:T(512)S(1)}, u32[]{:S(2)}) copy-start(f32[384]{0:T(512)S(1)} %get-tuple-element.1258) | copy-start | bytes 4612
  117.0 49.8 %copy-start.55 = (f32[256]{0:T(256)S(1)}, f32[256]{0:T(256)}, u32[]{:S(2)}) copy-start(f32[256]{0:T(256)} %param.39) | copy-start | bytes 3076
  141.7 25.2 %copy-start.17 = (bf16[1024,256]{1,0:T(8,128)(2,1)}, bf16[1024,256]{1,0:T(8,128)(2,1)S(1)}, u32[]{:S(2)}) copy-start(bf16[1024,256]{1,0:T(8,128)(2,1)S(1)} %all_gather.56) | copy-start | bytes 1572868
  142.2 24.7 %copy-start.13 = (f32[384,256]{0,1:T(8,128)}, f32[384,256]{0,1:T(8,128)S(1)}, u32[]{:S(2)}) copy-start(f32[384,256]{0,1:T(8,128)S(1)} %fusion.169) | copy-start | bytes 1179652
  169.9 69.7 %copy-start.1 = (bf16[384,1024]{1,0:T(8,128)(2,1)S(1)}, bf16[384,1024]{1,0:T(8,128)(2,1)}, u32[]{:S(2)}) copy-start(bf16[384,1024]{1,0:T(8,128)(2,1)} %param.27) | copy-start | bytes 2359300
  169.9 71.5 %copy-start.47 = (f32[1024]{0:T(1024)S(1)}, f32[1024]{0:T(1024)}, u32[]{:S(2)}) copy-start(f32[1024]{0:T(1024)} %param.40) | copy-start | bytes 12292
  169.9 72.7 %all-gather.6.cloned.1.call-start = ((), (), s32[]{:S(2)}) async-start(), calls=%async_computation.9 | async-start | bytes 1622016 | tf_op jit(solution)/shard_map/all_gather | solution.py:151
  170.5 76.3 %all-gather.8.cloned.1.call-start = ((), (), s32[]{:S(2)}) async-start(), calls=%async_computation.10 | async-start | bytes 1622016 | tf_op jit(solution)/shard_map/all_gather | solution.py:152
  171.1 80.5 %all-gather.10.cloned.1.call-start = ((), (), s32[]{:S(2)}) async-start(), calls=%async_computation.11 | async-start | bytes 1622016 | tf_op jit(solution)/shard_map/all_gather | solution.py:153
  171.7 157.2 %all-reduce.13.cloned.1.call-start = ((), (), s32[]{:S(2)}) async-start(), calls=%async_computation.12 | async-start | bytes 3145728 | tf_op jit(solution)/shard_map/psum | solution.py:205
  242.6 86.3 %copy-start.2 = (f32[384,1024]{1,0:T(8,128)}, f32[384,1024]{1,0:T(8,128)S(1)}, u32[]{:S(2)}) copy-start(f32[384,1024]{1,0:T(8,128)S(1)} %get-tuple-element.1230) | copy-start | bytes 4718596
  259.8 246.3 %all-reduce.15.cloned.1.call-start = ((), (), s32[]{:S(2)}) async-start(), calls=%async_computation.18 | async-start | bytes 131072 | tf_op jit(solution)/shard_map/psum | solution.py:274
  489.9 140.8 %all-reduce.19.cloned.1.call-start = ((), (), s32[]{:S(2)}) async-start(), calls=%async_computation.23 | async-start | bytes 6291456 | tf_op jit(solution)/shard_map/psum | solution.py:188
  494.4 247.8 %all-reduce.17.cloned.1.call-start = ((), (), s32[]{:S(2)}) async-start(), calls=%async_computation.19 | async-start | bytes 131072 | tf_op jit(solution)/shard_map/psum | solution.py:274
  506.1 236.1 %reduce-scatter.9.cloned.1.call-start = ((), (), s32[]{:S(2)}) async-start(), calls=%async_computation.13 | async-start | bytes 589824 | tf_op jit(solution)/shard_map/reduce_scatter | solution.py:278
  508.3 233.9 %reduce-scatter.11.cloned.1.call-start = ((), (), s32[]{:S(2)}) async-start(), calls=%async_computation.14 | async-start | bytes 589824 | tf_op jit(solution)/shard_map/reduce_scatter | solution.py:279
  510.5 231.8 %reduce-scatter.13.cloned.1.call-start = ((), (), s32[]{:S(2)}) async-start(), calls=%async_computation.15 | async-start | bytes 1179648 | tf_op jit(solution)/shard_map/reduce_scatter | solution.py:280
  513.0 229.3 %reduce-scatter.17.cloned.1.call-start = ((), (), s32[]{:S(2)}) async-start(), calls=%async_computation.17 | async-start | bytes 1179648 | tf_op jit(solution)/shard_map/reduce_scatter | solution.py:282
  515.4 226.8 %reduce-scatter.15.cloned.1.call-start = ((), (), s32[]{:S(2)}) async-start(), calls=%async_computation.16 | async-start | bytes 1179648 | tf_op jit(solution)/shard_map/reduce_scatter | solution.py:281
  517.2 233.9 %reduce-scatter.19.cloned.1.call-start = ((), (), s32[]{:S(2)}) async-start(), calls=%async_computation.20 | async-start | bytes 3244032 | tf_op jit(solution)/shard_map/reduce_scatter | solution.py:283
  521.9 277.8 %reduce-scatter.21.cloned.1.call-start = ((), (), s32[]{:S(2)}) async-start(), calls=%async_computation.21 | async-start | bytes 3244032 | tf_op jit(solution)/shard_map/reduce_scatter | solution.py:284
  525.5 322.5 %reduce-scatter.23.cloned.1.call-start = ((), (), s32[]{:S(2)}) async-start(), calls=%async_computation.22 | async-start | bytes 3244032 | tf_op jit(solution)/shard_map/reduce_scatter | solution.py:285
  530.3 101.6 %copy-start.57 = (f32[256]{0:T(256)S(1)}, f32[256]{0:T(256)}, u32[]{:S(2)}) copy-start(f32[256]{0:T(256)} %get-tuple-element.1105) | copy-start | bytes 3076
  530.3 182.4 %copy-start.46 = (f32[1024]{0:T(1024)S(1)}, f32[1024]{0:T(1024)}, u32[]{:S(2)}) copy-start(f32[1024]{0:T(1024)} %param.30) | copy-start | bytes 12292
  (46 other events, 136.0 us)
Sparse Core Ops, SparseCore 0:
  170.0 69.4 all-reduce.10
  259.9 68.9 all-reduce.12
  490.0 16.0 all-reduce.14
  508.4 122.2 all-reduce.18
  636.0 106.1 all-reduce.16
Sparse Core Ops, SparseCore 1:
  172.3 25.5 all-gather.5
  199.6 25.0 all-gather.7
  226.5 25.0 all-gather.9
  510.6 35.3 reduce-scatter.8
  549.6 34.0 reduce-scatter.10
  587.5 35.9 reduce-scatter.12
  627.0 35.9 reduce-scatter.16
  666.7 35.9 reduce-scatter.14
  706.5 44.5 reduce-scatter.18
  755.1 44.5 reduce-scatter.20
  803.5 44.5 reduce-scatter.22
